TPU v7x, 32 devices: a whole 2x2x4 slice. The times are simulated.
32 devices in a mesh: dp: 2 (over x), expert: 16 (over z, y, core).
Axes of the slice: x: 2, y: 2, z: 4, core: 2. Of those that a mesh axis runs over, the one named last changes fastest.
Arguments:
- tokens: bfloat16 [4096, 2048], P(('dp', 'expert')), may hold values from -6 to 6
- gate_weights: float32 [4096, 2], P(('dp', 'expert')), may hold values from 0.02 to 0.5
- expert_ids: int32 [4096, 2], P(('dp', 'expert')), may hold values from 0 to 15, as said below
- hot_experts: int32 [4], replicated, may hold values from 0 to 15, as said below
- gate_proj: bfloat16 [16, 2048, 768], P('expert', 'dp'), may hold values from -0.125 to 0.125
- up_proj: bfloat16 [16, 2048, 768], P('expert', 'dp'), may hold values from -0.125 to 0.125
- down_proj: bfloat16 [16, 2048, 768], P('expert', 'dp'), may hold values from -0.21875 to 0.21875
- out_grad: bfloat16 [4096, 2048], P(('dp', 'expert')), may hold values from -6 to 6
Outputs:
- layer_out: bfloat16 [4096, 2048], P(('dp', 'expert'))
- tokens_grad: bfloat16 [4096, 2048], P(('dp', 'expert'))
- routing_grad: float32 [4096, 2], P(('dp', 'expert'))
- gate_proj_grad: bfloat16 [16, 2048, 768], P('expert', 'dp')
- up_proj_grad: bfloat16 [16, 2048, 768], P('expert', 'dp')
- down_proj_grad: bfloat16 [16, 2048, 768], P('expert', 'dp')
Inputs may be any that keep to these rules, and one draw needn't show every extreme that they name: `expert_ids`: each token names 2 different experts. In each block of 128 rows of one device no expert is named more than 28 times, and the expert hot_experts[0] is named exactly 28 times in every block. `hot_experts`: 4 different experts.
All inputs are finite; a program needn't handle non-finite values.
Results may differ from a plain program's by a relative error of at most 0.012.
Values may be sent and summed in bfloat16 or wider, within the bound.
No kernel may reach another device: no remote copies, remote signals or barrier semaphores. Data moves between devices by JAX's collectives and lax.ppermute only.
A program may use at most 128 MiB of HBM per device.

v0:
```python
import jax
import jax.numpy as jnp
from jax import lax
from jax.sharding import PartitionSpec as P

TOPK = 2


def contract_last(left_side, right_side):
    return lax.dot_general(
        left_side, right_side, (((1,), (1,)), ((), ())), preferred_element_type=jnp.float32
    )


def contract_first(left_side, right_side):
    return lax.dot_general(
        left_side, right_side, (((0,), (0,)), ((), ())), preferred_element_type=jnp.float32
    )


def body(tokens, gate_weights, expert_ids, hot_experts, gate_proj, up_proj, down_proj, out_grad):
    owners = lax.axis_size("expert")
    model_width = tokens.shape[1]
    token_count = tokens.shape[0]
    assign_count = token_count * TOPK
    cap_rows = 5 * assign_count // (4 * owners)
    slot_count = cap_rows + assign_count // (2 * owners)
    local_gate = gate_proj[0]
    local_up = up_proj[0]
    local_down = down_proj[0]
    hidden_units = local_gate.shape[1]
    flat_ids = expert_ids.reshape(-1)
    expert_range = jnp.arange(owners, dtype=jnp.int32)
    onehot = (flat_ids[:, None] == expert_range[None, :]).astype(jnp.int32)
    before = jnp.cumsum(onehot, axis=0) - onehot
    slot_pos = jnp.sum(before * onehot, axis=1)
    hot_flags = jnp.sum((hot_experts[:, None] == expert_range[None, :]).astype(jnp.int32), axis=0)
    hot_row = jnp.sum(onehot * hot_flags[None, :], axis=1) > 0
    kept_mask = slot_pos < jnp.where(hot_row, slot_count, cap_rows)
    row_slot = flat_ids * slot_count + jnp.minimum(slot_pos, slot_count - 1)
    target = jnp.where(kept_mask, row_slot, -1)
    placing = (jnp.arange(owners * slot_count, dtype=jnp.int32)[:, None] == target[None, :]).astype(
        jnp.bfloat16
    )
    token_place = placing.reshape(owners * slot_count, token_count, TOPK).sum(axis=2)
    send_rows = jnp.dot(token_place, tokens, preferred_element_type=jnp.float32).astype(
        jnp.bfloat16
    )
    send_rows = send_rows.reshape(owners, slot_count, model_width)
    received = lax.all_to_all(send_rows, "expert", split_axis=0, concat_axis=0, tiled=True)
    expert_expert_rows = received.reshape(-1, model_width)
    pieces = (
        lax.all_gather(local_gate, "dp", axis=0, tiled=True),
        lax.all_gather(local_up, "dp", axis=0, tiled=True),
    )
    columns = expert_expert_rows
    gate_act = jnp.dot(columns, pieces[0], preferred_element_type=jnp.float32)
    up_act = jnp.dot(columns, pieces[1], preferred_element_type=jnp.float32)
    expert_hidden = (gate_act * jax.nn.sigmoid(gate_act) * up_act).astype(jnp.bfloat16)
    output = contract_last(
        expert_hidden, lax.all_gather(local_down, "dp", axis=0, tiled=True)
    ).astype(jnp.bfloat16)
    returned = lax.all_to_all(
        output.reshape(received.shape), "expert", split_axis=0, concat_axis=0, tiled=True
    )
    act_shape = (received.shape[0], received.shape[1], hidden_units)
    returned, saved_rows, saved_gate, saved_up = (
        returned,
        received,
        gate_act.reshape(act_shape),
        up_act.reshape(act_shape),
    )
    safe_slot = jnp.where(kept_mask, row_slot, 0)
    keep_scale = kept_mask.astype(jnp.float32)[:, None]
    chosen = (
        jnp.take(returned.reshape(-1, model_width), safe_slot, axis=0).astype(jnp.float32)
        * keep_scale
    )
    weight_flat = gate_weights.reshape(-1, 1)
    layer_out = (
        (chosen * weight_flat)
        .reshape(token_count, TOPK, model_width)
        .sum(axis=1)
        .astype(jnp.bfloat16)
    )
    routing_grad = jnp.sum(
        chosen.reshape(token_count, TOPK, model_width) * out_grad.astype(jnp.float32)[:, None, :],
        axis=2,
    )
    spread = (weight_flat * jnp.repeat(out_grad, TOPK, axis=0).astype(jnp.float32)).astype(
        jnp.bfloat16
    )
    grad_send = jnp.dot(placing, spread, preferred_element_type=jnp.float32).astype(jnp.bfloat16)
    grad_recv = lax.all_to_all(
        grad_send.reshape(owners, slot_count, model_width),
        "expert",
        split_axis=0,
        concat_axis=0,
        tiled=True,
    )
    grad_in = grad_recv.reshape(-1, model_width)
    expert_rows = saved_rows.reshape(-1, model_width)
    gate_act = saved_gate.reshape(-1, hidden_units)
    up_act = saved_up.reshape(-1, hidden_units)
    columns = grad_in
    grad_hidden = jnp.dot(
        columns,
        lax.all_gather(local_down, "dp", axis=0, tiled=True),
        preferred_element_type=jnp.float32,
    )
    sigmoid_act = jax.nn.sigmoid(gate_act)
    silu_act = gate_act * sigmoid_act
    hidden = (silu_act * up_act).astype(jnp.bfloat16)
    grad_up = (grad_hidden * silu_act).astype(jnp.bfloat16)
    grad_gate = (
        grad_hidden * up_act * sigmoid_act * (1.0 + gate_act * (1.0 - sigmoid_act))
    ).astype(jnp.bfloat16)
    pieces = lax.all_gather((local_gate, local_up), "dp", axis=0, tiled=True)
    grad_rows = (contract_last(grad_gate, pieces[0]) + contract_last(grad_up, pieces[1])).astype(
        jnp.bfloat16
    )
    grad_back = lax.all_to_all(
        grad_rows.reshape(owners, slot_count, model_width),
        "expert",
        split_axis=0,
        concat_axis=0,
        tiled=True,
    )
    chosen_grad = (
        jnp.take(grad_back.reshape(-1, model_width), safe_slot, axis=0).astype(jnp.float32)
        * keep_scale
    )
    tokens_grad = (
        chosen_grad.reshape(token_count, TOPK, model_width).sum(axis=1).astype(jnp.bfloat16)
    )
    summed = lax.psum_scatter(
        jnp.concatenate(
            [
                contract_first(expert_rows, grad_gate),
                contract_first(expert_rows, grad_up),
                contract_first(grad_in, hidden),
            ],
            axis=1,
        ).astype(jnp.bfloat16),
        "dp",
        scatter_dimension=0,
        tiled=True,
    ).astype(jnp.float32)
    gate_proj_grad = summed[:, :hidden_units].astype(jnp.bfloat16)[None]
    up_proj_grad = summed[:, hidden_units : 2 * hidden_units].astype(jnp.bfloat16)[None]
    down_proj_grad = summed[:, 2 * hidden_units :].astype(jnp.bfloat16)[None]
    return (layer_out, tokens_grad, routing_grad, gate_proj_grad, up_proj_grad, down_proj_grad)


def solution(mesh):
    in_specs = (
        P(("dp", "expert"), None),
        P(("dp", "expert"), None),
        P(("dp", "expert"), None),
        P(),
        P("expert", "dp", None),
        P("expert", "dp", None),
        P("expert", "dp", None),
        P(("dp", "expert"), None),
    )
    out_specs = (
        P(("dp", "expert"), None),
        P(("dp", "expert"), None),
        P(("dp", "expert"), None),
        P("expert", "dp", None),
        P("expert", "dp", None),
        P("expert", "dp", None),
    )
    return jax.shard_map(body, mesh=mesh, in_specs=in_specs, out_specs=out_specs, check_vma=False)
```

profile of v0, /device:TPU:13, one launch (start us, length us, event | category | flops | bytes accessed | tf_op | source)
XLA Modules:
  0.0 318.9 jit_solution(3125575328886771847)
XLA Ops:
  9.0 2.4 broadcast_in_dim.51
  11.4 2.7 convert_element_type.84
  17.4 3.7 %reshape.124 = bf16[16,28,2048]{2,1,0:T(8,128)(2,1)} reshape(bf16[448,2048]{1,0:T(8,128)(2,1)} %convolution_convert_fusion.3) | data formatting | bytes 3670016 | tf_op jit(solution)/shard_map/reshape | solution.py:95
  21.1 6.7 %all-to-all-start.2 = ((bf16[16,28,2048]{2,1,0:T(8,128)(2,1)}), bf16[16,28,2048]{2,1,0:T(8,128)(2,1)S(1)}, u32[]{:S(2)}, u32[]{:S(2)}) async-start(bf16[16,28,2048]{2,1,0:T(8,128)(2,1)} %reshape.124), calls=%async_computation.2 | async-start | bytes 4194304 | tf_op jit(solution)/shard_map/all_to_all | solution.py:94
  31.0 3.5 %reshape.119 = bf16[16,28,2048]{2,1,0:T(8,128)(2,1)} reshape(bf16[448,2048]{1,0:T(8,128)(2,1)} %convolution_convert_fusion.4) | data formatting | bytes 3670016 | tf_op jit(solution)/shard_map/reshape | solution.py:49
  34.5 41.1 %all-to-all-done.2 = bf16[16,28,2048]{2,1,0:T(8,128)(2,1)S(1)} async-done(((bf16[16,28,2048]{2,1,0:T(8,128)(2,1)}), bf16[16,28,2048]{2,1,0:T(8,128)(2,1)S(1)}, u32[]{:S(2)}, u32[]{:S(2)}) %all-to-all-start.2) | async-done | bytes 1835040 | tf_op jit(solution)/shard_map/all_to_all | solution.py:94
  75.6 4.4 %all-to-all-start = ((bf16[16,28,2048]{2,1,0:T(8,128)(2,1)}), bf16[16,28,2048]{2,1,0:T(8,128)(2,1)}, u32[]{:S(2)}, u32[]{:S(2)}) async-start(bf16[16,28,2048]{2,1,0:T(8,128)(2,1)} %reshape.119), calls=%async_computation | async-start | bytes 4194304 | tf_op jit(solution)/shard_map/all_to_all | solution.py:50
  82.4 45.4 %all-to-all-done = bf16[16,28,2048]{2,1,0:T(8,128)(2,1)} async-done(((bf16[16,28,2048]{2,1,0:T(8,128)(2,1)}), bf16[16,28,2048]{2,1,0:T(8,128)(2,1)}, u32[]{:S(2)}, u32[]{:S(2)}) %all-to-all-start) | async-done | bytes 1835040 | tf_op jit(solution)/shard_map/all_to_all | solution.py:50
  127.8 3.6 %reshape.120 = bf16[448,2048]{1,0:T(8,128)(2,1)} reshape(bf16[16,28,2048]{2,1,0:T(8,128)(2,1)} %all-to-all-done) | data formatting | bytes 3670016 | tf_op jit(solution)/shard_map/reshape | solution.py:51
  131.4 4.6 %fusion = f32[448,768]{1,0:T(8,128)} fusion(bf16[448,2048]{1,0:T(8,128)(2,1)S(1)} %copy-done.5, bf16[1,2048,768]{2,1,0:T(8,128)(2,1)} %all-gather.11.cloned.1.call-done), kind=kOutput, calls=%fused_computation.7 | convolution fusion | flops 1409286144 | bytes 6356992 | tf_op jit(solution)/shard_map/dot_general | solution.py:106
  136.0 5.1 %fusion.6 = f32[448,768]{1,0:T(8,128)} fusion(bf16[448,2048]{1,0:T(8,128)(2,1)} %reshape.120, bf16[1,2048,768]{2,1,0:T(8,128)(2,1)} %all-gather.9.cloned.1.call-done), kind=kOutput, calls=%fused_computation.13 | convolution fusion | flops 1409286144 | bytes 6356992 | tf_op jit(solution)/shard_map/dot_general | solution.py:58
  141.1 7.4 %all-gather.7.cloned.1.call-done = bf16[1,2048,768]{2,1,0:T(8,128)(2,1)} async-done(((bf16[1,1024,768]{2,1,0:T(8,128)(2,1)}), bf16[1,2048,768]{2,1,0:T(8,128)(2,1)}) %all-gather.7.cloned.1.call-update) | async-done | bytes 3145744 | tf_op jit(solution)/shard_map/all_gather | solution.py:53
  148.4 5.3 %multiply_convert_fusion.2 = (bf16[448,768]{1,0:T(8,128)(2,1)S(1)}, bf16[448,768]{1,0:T(8,128)(2,1)S(1)}, bf16[448,768]{1,0:T(8,128)(2,1)S(1)}) fusion(f32[448,768]{1,0:T(8,128)} %fusion, f32[448,768]{1,0:T(8,128)} %fusion.6, bf16[448,2048]{1,0:T(8,128)(2,1)} %reshape.120, bf16[1,2048,768]{2,1,0:T(8,128)(2,1)} %all-gather.7.cloned.1.call-done), kind=kOutput, calls=%fused_computation.31 | convolution fusion | flops 1414447104 | bytes 9797632 | tf_op jit(solution)/shard_map/dot_general | solution.py:57
  159.5 4.5 %pad_maximum_fusion = bf16[2048,2304]{0,1:T(8,128)(2,1)} fusion(bf16[2048,768]{0,1:T(8,128)(2,1)S(1)} %convolution_convert_fusion, bf16[2048,768]{0,1:T(8,128)(2,1)S(1)} %convolution_convert_fusion.1, bf16[2048,768]{0,1:T(8,128)(2,1)S(1)} %convolution_convert_fusion.2), kind=kLoop, calls=%fused_computation.2 | loop fusion | flops 28311552 | bytes 18874368 | tf_op jit(solution)/shard_map/concatenate | solution.py:137
  164.0 3.7 %fusion.12 = bf16[448,2048]{1,0:T(8,128)(2,1)S(1)} fusion(bf16[448,768]{1,0:T(8,128)(2,1)} %copy-done.12, bf16[1,2048,768]{2,1,0:T(8,128)(2,1)} %all-gather.11.cloned.1.call-done), kind=kOutput, calls=%fused_computation.21 | convolution fusion | flops 1410203648 | bytes 5668864 | tf_op jit(solution)/shard_map/dot_general | solution.py:10
  169.3 6.5 %all-to-all-start.1 = ((bf16[16,28,2048]{2,1,0:T(8,128)(2,1)}), bf16[16,28,2048]{2,1,0:T(8,128)(2,1)S(1)}, u32[]{:S(2)}, u32[]{:S(2)}) async-start(bf16[16,28,2048]{2,1,0:T(8,128)(2,1)} %reshape.121), calls=%async_computation.1 | async-start | bytes 4194304 | tf_op jit(solution)/shard_map/all_to_all | solution.py:63
  175.8 3.7 %fusion.4 = f32[448,2048]{1,0:T(8,128)S(1)} fusion(bf16[448,768]{1,0:T(8,128)(2,1)S(1)} %get-tuple-element.41, bf16[1,2048,768]{2,1,0:T(8,128)(2,1)} %all-gather.9.cloned.1.call-done), kind=kOutput, calls=%fused_computation.11 | convolution fusion | flops 1409286144 | bytes 7503872 | tf_op jit(solution)/shard_map/dot_general | solution.py:10
  179.5 2.9 add_convert_fusion
  182.3 3.5 %reshape.126 = bf16[16,28,2048]{2,1,0:T(8,128)(2,1)} reshape(bf16[448,2048]{1,0:T(8,128)(2,1)} %add_convert_fusion) | data formatting | bytes 3670016 | tf_op jit(solution)/shard_map/reshape | solution.py:123
  185.9 37.7 %all-to-all-done.1 = bf16[16,28,2048]{2,1,0:T(8,128)(2,1)S(1)} async-done(((bf16[16,28,2048]{2,1,0:T(8,128)(2,1)}), bf16[16,28,2048]{2,1,0:T(8,128)(2,1)S(1)}, u32[]{:S(2)}, u32[]{:S(2)}) %all-to-all-start.1) | async-done | bytes 1835040 | tf_op jit(solution)/shard_map/all_to_all | solution.py:63
  224.9 4.6 %all-to-all-start.3 = ((bf16[16,28,2048]{2,1,0:T(8,128)(2,1)}), bf16[16,28,2048]{2,1,0:T(8,128)(2,1)}, u32[]{:S(2)}, u32[]{:S(2)}) async-start(bf16[16,28,2048]{2,1,0:T(8,128)(2,1)} %reshape.126), calls=%async_computation.3 | async-start | bytes 4194304 | tf_op jit(solution)/shard_map/all_to_all | solution.py:122
  229.5 2.6 reshape.122
  232.1 2.3 gather_fusion
  234.4 42.4 %all-to-all-done.3 = bf16[16,28,2048]{2,1,0:T(8,128)(2,1)} async-done(((bf16[16,28,2048]{2,1,0:T(8,128)(2,1)}), bf16[16,28,2048]{2,1,0:T(8,128)(2,1)}, u32[]{:S(2)}, u32[]{:S(2)}) %all-to-all-start.3) | async-done | bytes 1835040 | tf_op jit(solution)/shard_map/all_to_all | solution.py:122
  276.8 2.5 reshape.127
  281.6 4.2 %multiply_reduce_fusion = (f32[256]{0:T(256)S(1)}, f32[256,2048]{1,0:T(8,128)}, f32[256,2048]{1,0:T(8,128)S(1)}) fusion(f32[256,2048]{1,0:T(8,128)} %copy-done.2, f32[256]{0:T(256)S(1)} %get-tuple-element.47, bf16[256,2048]{1,0:T(8,128)(2,1)} %gather_fusion, pred[256]{0:T(512)(128)(4,1)S(1)} %get-tuple-element.35, f32[256]{0:T(256)S(1)} %mul.91, ...), kind=kLoop, calls=%fused_computation.22 | loop fusion | flops 4718336 | bytes 8391936 | tf_op jit(solution)/shard_map/reduce_sum | solution.py:86
  285.8 3.4 %reshape.123 = f32[128,2,2048]{2,1,0:T(2,128)} reshape(f32[256,2048]{1,0:T(8,128)} %get-tuple-element.44) | data formatting | bytes 4194304 | tf_op jit(solution)/shard_map/reshape | solution.py:82
  291.4 5.1 %reduce_sum.72 = bf16[128,2048]{1,0:T(8,128)(2,1)} reduce(f32[128,2,2048]{2,1,0:T(2,128)} %reshape.123, f32[]{:T(128)} %constant.32.clone.1), dimensions={1}, to_apply=%region_6.8 | reduce | flops 262144 | bytes 2621444 | tf_op jit(solution)/shard_map/reduce_sum | solution.py:83
  296.5 3.8 %reduce_sum.73 = bf16[128,2048]{1,0:T(8,128)(2,1)} reduce(f32[128,2,2048]{2,1,0:T(2,128)S(1)} %copy-done.4, f32[]{:T(128)} %constant.32.clone.1), dimensions={1}, to_apply=%region_7.9 | reduce | flops 262144 | bytes 2621444 | tf_op jit(solution)/shard_map/reduce_sum | solution.py:134
  301.1 4.5 %slice_bitcast_fusion = (bf16[1,1024,768]{1,2,0:T(8,128)(2,1)S(1)}, bf16[1,1024,768]{1,2,0:T(8,128)(2,1)}, bf16[1,1024,768]{1,2,0:T(8,128)(2,1)}) fusion(bf16[1024,2304]{0,1:T(8,128)(2,1)} %reduce-scatter.2.cloned.1.call-done), kind=kLoop, calls=%fused_computation.27 | loop fusion | bytes 9437184 | tf_op jit(solution)/shard_map/broadcast_in_dim | solution.py:151
  305.6 2.6 copy.46
  308.2 2.6 copy.47
  (74 shorter events, 26.1 us)
Async XLA Ops:
  7.2 21.9 %copy-start = (bf16[128,2048]{1,0:T(8,128)(2,1)S(1)}, bf16[128,2048]{1,0:T(8,128)(2,1)}, u32[]{:S(2)}) copy-start(bf16[128,2048]{1,0:T(8,128)(2,1)} %param.10) | copy-start | bytes 1572868
  7.2 1.8 copy-start.7
  7.2 124.2 %all-gather.11.cloned.1.call-start = ((), (), s32[]{:S(2)}) async-start(), calls=%async_computation.8 | async-start | bytes 4718592 | tf_op jit(solution)/shard_map/all_gather | solution.py:61
  11.4 3.6 %copy-start.9 = (f32[128,2]{0,1:T(2,128)S(1)}, f32[128,2]{0,1:T(2,128)}, u32[]{:S(2)}) copy-start(f32[128,2]{0,1:T(2,128)} %param.11) | copy-start | bytes 3076
  11.4 3.8 %copy-start.11 = (s32[4]{0:T(128)S(1)}, s32[4]{0:T(128)}, u32[]{:S(2)}) copy-start(s32[4]{0:T(128)} %param.13) | copy-start | bytes 52
  14.1 7.0 %copy-start.2 = (f32[256,2048]{1,0:T(8,128)}, f32[256,2048]{1,0:T(8,128)S(1)}, u32[]{:S(2)}) copy-start(f32[256,2048]{1,0:T(8,128)S(1)} %convert_element_type.84) | copy-start | bytes 6291460
  21.1 7.9 %copy-start.8 = (s32[128,2]{0,1:T(2,128)S(1)}, s32[128,2]{0,1:T(2,128)}, u32[]{:S(2)}) copy-start(s32[128,2]{0,1:T(2,128)} %param.12) | copy-start | bytes 3076
  21.1 54.5 %all-to-all-start.2 = ((bf16[16,28,2048]{2,1,0:T(8,128)(2,1)}), bf16[16,28,2048]{2,1,0:T(8,128)(2,1)S(1)}, u32[]{:S(2)}, u32[]{:S(2)}) async-start(bf16[16,28,2048]{2,1,0:T(8,128)(2,1)} %reshape.124), calls=%async_computation.2 | async-start | bytes 4194304 | tf_op jit(solution)/shard_map/all_to_all | solution.py:94
  27.8 108.2 %all-gather.9.cloned.1.call-start = ((), (), s32[]{:S(2)}) async-start(), calls=%async_computation.7 | async-start | bytes 4718592 | tf_op jit(solution)/shard_map/all_gather | solution.py:54
  75.6 52.2 %all-to-all-start = ((bf16[16,28,2048]{2,1,0:T(8,128)(2,1)}), bf16[16,28,2048]{2,1,0:T(8,128)(2,1)}, u32[]{:S(2)}, u32[]{:S(2)}) async-start(bf16[16,28,2048]{2,1,0:T(8,128)(2,1)} %reshape.119), calls=%async_computation | async-start | bytes 4194304 | tf_op jit(solution)/shard_map/all_to_all | solution.py:50
  80.0 68.4 %all-gather.7.cloned.1.call-start = ((), (), s32[]{:S(2)}) async-start(), calls=%async_computation.6 | async-start | bytes 4718592 | tf_op jit(solution)/shard_map/all_gather | solution.py:53
  80.7 220.4 %reduce-scatter.2.cloned.1.call-start = ((), (), s32[]{:S(2)}) async-start(), calls=%async_computation.5 | async-start | bytes 14155776 | tf_op jit(solution)/shard_map/reduce_scatter | solution.py:136
  82.4 49.0 %copy-start.5 = (bf16[448,2048]{1,0:T(8,128)(2,1)S(1)}, bf16[448,2048]{1,0:T(8,128)(2,1)}, u32[]{:S(2)}) copy-start(bf16[448,2048]{1,0:T(8,128)(2,1)} %reshape.125) | copy-start | bytes 5505028
  153.7 1.9 copy-start.12
  153.7 3.9 %copy-start.13 = (bf16[448,768]{1,0:T(8,128)(2,1)}, bf16[448,768]{1,0:T(8,128)(2,1)S(1)}, u32[]{:S(2)}) copy-start(bf16[448,768]{1,0:T(8,128)(2,1)S(1)} %get-tuple-element.40) | copy-start | bytes 2064388
  153.7 2.0 copy-start.6
  169.3 54.3 %all-to-all-start.1 = ((bf16[16,28,2048]{2,1,0:T(8,128)(2,1)}), bf16[16,28,2048]{2,1,0:T(8,128)(2,1)S(1)}, u32[]{:S(2)}, u32[]{:S(2)}) async-start(bf16[16,28,2048]{2,1,0:T(8,128)(2,1)} %reshape.121), calls=%async_computation.1 | async-start | bytes 4194304 | tf_op jit(solution)/shard_map/all_to_all | solution.py:63
  175.8 3.7 %copy-start.10 = (bf16[1,2048,768]{2,1,0:T(8,128)(2,1)S(1)}, bf16[1,2048,768]{2,1,0:T(8,128)(2,1)}, u32[]{:S(2)}) copy-start(bf16[1,2048,768]{2,1,0:T(8,128)(2,1)} %all-gather.7.cloned.1.call-done) | copy-start | bytes 9437188
  175.8 3.7 %copy-start.14 = (bf16[448,768]{1,0:T(8,128)(2,1)S(1)}, bf16[448,768]{1,0:T(8,128)(2,1)}, u32[]{:S(2)}) copy-start(bf16[448,768]{1,0:T(8,128)(2,1)} %copy-done.13) | copy-start | bytes 2064388
  223.6 1.3 copy-start.3
  224.9 51.9 %all-to-all-start.3 = ((bf16[16,28,2048]{2,1,0:T(8,128)(2,1)}), bf16[16,28,2048]{2,1,0:T(8,128)(2,1)}, u32[]{:S(2)}, u32[]{:S(2)}) async-start(bf16[16,28,2048]{2,1,0:T(8,128)(2,1)} %reshape.126), calls=%async_computation.3 | async-start | bytes 4194304 | tf_op jit(solution)/shard_map/all_to_all | solution.py:122
  291.4 5.1 %copy-start.4 = (f32[128,2,2048]{2,1,0:T(2,128)S(1)}, f32[128,2,2048]{2,1,0:T(2,128)}, u32[]{:S(2)}) copy-start(f32[128,2,2048]{2,1,0:T(2,128)} %reshape.128) | copy-start | bytes 6291460
  308.2 4.2 %copy-start.1 = (bf16[128,2048]{1,0:T(8,128)(2,1)S(1)}, bf16[128,2048]{1,0:T(8,128)(2,1)}, u32[]{:S(2)}) copy-start(bf16[128,2048]{1,0:T(8,128)(2,1)} %param.10) | copy-start | bytes 1572868
Sparse Core Ops, SparseCore 0:
  9.5 45.8 all-gather.10
  57.0 44.8 all-gather.8
  103.5 44.8 all-gather.6
  164.1 110.6 reduce-scatter.1
where the time goes:
time: 320 us; the launch traced here: 319 us
  waiting for transfers between devices  176 us (55%)
  local copies, waits for them, and re-layouts  53.2 us (17%)
  matrix products  34.7 us (11%)
  starting transfers between devices  22.4 us (7%)
  other arithmetic  18.4 us (6%)
  between operations  14 us (4%)
    all_to_all x1, waiting for transfers between devices, body(): lax.all_to_all(send_rows, 'expert', split_axis=0, concat_axis=0, tiled=True)  45.4 us
    all_to_all x1, waiting for transfers between devices, body(): lax.all_to_all(grad_rows.reshape(owners, slot_count, model_width), 'exper...  42.4 us
    all_to_all x1, waiting for transfers between devices, body(): lax.all_to_all(grad_send.reshape(owners, slot_count, model_width), 'exper...  41.1 us
    all_to_all x1, waiting for transfers between devices, body(): lax.all_to_all(output.reshape(received.shape), 'expert', split_axis=0, co...  37.7 us
    dot_general x3, matrix products, contract_last(): lax.dot_general(left_side, right_side, (((1,), (1,)), ((), ())), preferre...  10.3 us
    unnamed x36, local copies, waits for them, and re-layouts  9.8 us
    all_gather x1, waiting for transfers between devices, body(): lax.all_gather(local_gate, 'dp', axis=0, tiled=True)  7.35 us
    all_to_all x1, starting transfers between devices, body(): lax.all_to_all(grad_send.reshape(owners, slot_count, model_width), 'exper...  6.66 us
  transfers between devices with their start and end apart: 8, of which 5 were waited for; matrix products, arithmetic and copies ran while one was open for 25% of the time, Pallas kernels for 0%

commit v1 on v0

--- a/solution.py
+++ b/solution.py
@@ -4,6 +4,22 @@
 from jax.sharding import PartitionSpec as P
 
 TOPK = 2
+
+
+def exchange_in_pairs(x, axis, split, join):
+    ways, here = (lax.axis_size(axis), lax.axis_index(axis))
+    width = x.shape[split] // ways
+    shape = list(x.shape)
+    shape[split] = width
+    height = shape[join]
+    shape[join] = height * ways
+    full = jnp.zeros(shape, x.dtype)
+    for mask in range(ways):
+        part = lax.dynamic_slice_in_dim(x, (here ^ mask) * width, width, axis=split)
+        if mask:
+            part = lax.ppermute(part, axis, [(d, d ^ mask) for d in range(ways)])
+        full = lax.dynamic_update_slice_in_dim(full, part, (here ^ mask) * height, axis=join)
+    return full
 
 
 def contract_last(left_side, right_side):
@@ -119,12 +135,8 @@
     grad_rows = (contract_last(grad_gate, pieces[0]) + contract_last(grad_up, pieces[1])).astype(
         jnp.bfloat16
     )
-    grad_back = lax.all_to_all(
-        grad_rows.reshape(owners, slot_count, model_width),
-        "expert",
-        split_axis=0,
-        concat_axis=0,
-        tiled=True,
+    grad_back = exchange_in_pairs(
+        grad_rows.reshape(owners, slot_count, model_width), "expert", 0, 0
     )
     chosen_grad = (
         jnp.take(grad_back.reshape(-1, model_width), safe_slot, axis=0).astype(jnp.float32)

time: 320 us -> 330 us (1.031)
  starting transfers between devices: 22.4 us -> 42.7 us
  waiting for transfers between devices: 176 us -> 156 us
  local copies, waits for them, and re-layouts: 53.2 us -> 63.9 us
    ppermute x0 -> x15, waiting for transfers between devices: none -> 60 us  [exchange_in_pairs(): part = lax.ppermute(part, axis, [(d, d ^ mask) for d in range(ways)])]
    all_to_all x1 -> x0, waiting for transfers between devices: 42.4 us -> none  [body(): lax.all_to_all(grad_rows.reshape(owners, slot_count, model_width), 'exper...]
    all_to_all x1, waiting for transfers between devices: 37.7 us -> 0.01 us  [body(): lax.all_to_all(output.reshape(received.shape), 'expert', split_axis=0, co...]
    ppermute x0 -> x15, starting transfers between devices: none -> 24.8 us  [exchange_in_pairs(): part = lax.ppermute(part, axis, [(d, d ^ mask) for d in range(ways)])]
    dynamic_update_slice x0 -> x15, local copies, waits for them, and re-layouts: none -> 9.85 us  [exchange_in_pairs(): lax.dynamic_update_slice_in_dim(full, part, (here ^ mask) * height, axis=...]
    all_to_all x1 -> x0, starting transfers between devices: 4.56 us -> none  [body(): lax.all_to_all(grad_rows.reshape(owners, slot_count, model_width), 'exper...]
    unnamed x36 -> x46, local copies, waits for them, and re-layouts: 9.8 us -> 9.11 us
  transfers between devices with their start and end apart: 8 -> 22, of which waited for: 5 -> 14; matrix products, arithmetic and copies ran while one was open for 25% -> 27% of each run, Pallas kernels for 0% -> 0%
where the time goes in v1:
time: 330 us; the launch traced here: 328 us
  waiting for transfers between devices  156 us (47%)
  local copies, waits for them, and re-layouts  63.9 us (19%)
  starting transfers between devices  42.7 us (13%)
  matrix products  32.6 us (10%)
  other arithmetic  18.9 us (6%)
  between operations  14.2 us (4%)
    ppermute x15, waiting for transfers between devices, exchange_in_pairs(): part = lax.ppermute(part, axis, [(d, d ^ mask) for d in range(ways)])  60 us
    all_to_all x1, waiting for transfers between devices, body(): lax.all_to_all(send_rows, 'expert', split_axis=0, concat_axis=0, tiled=True)  45.4 us
    all_to_all x1, waiting for transfers between devices, body(): lax.all_to_all(grad_send.reshape(owners, slot_count, model_width), 'exper...  41.1 us
    ppermute x15, starting transfers between devices, exchange_in_pairs(): part = lax.ppermute(part, axis, [(d, d ^ mask) for d in range(ways)])  24.8 us
    dynamic_update_slice x15, local copies, waits for them, and re-layouts, exchange_in_pairs(): lax.dynamic_update_slice_in_dim(full, part, (here ^ mask) * height, axis=...  9.85 us
    unnamed x46, local copies, waits for them, and re-layouts  9.11 us
    dot_general x3, matrix products, contract_last(): lax.dot_general(left_side, right_side, (((1,), (1,)), ((), ())), preferre...  8.18 us
    all_gather x1, waiting for transfers between devices, body(): lax.all_gather(local_gate, 'dp', axis=0, tiled=True)  7.35 us
  transfers between devices with their start and end apart: 22, of which 14 were waited for; matrix products, arithmetic and copies ran while one was open for 27% of the time, Pallas kernels for 0%

profile of v1, /device:TPU:13, one launch (start us, length us, event | category | flops | bytes accessed | tf_op | source)
XLA Modules:
  0.0 328.2 jit_solution(7709053384240778906)
XLA Ops:
  11.4 2.7 convert_element_type.84
  17.4 3.7 %reshape.124 = bf16[16,28,2048]{2,1,0:T(8,128)(2,1)} reshape(bf16[448,2048]{1,0:T(8,128)(2,1)} %convolution_convert_fusion.3) | data formatting | bytes 3670016 | tf_op jit(solution)/shard_map/reshape | solution.py:111
  21.1 6.7 %all-to-all-start.2 = ((bf16[16,28,2048]{2,1,0:T(8,128)(2,1)}), bf16[16,28,2048]{2,1,0:T(8,128)(2,1)S(1)}, u32[]{:S(2)}, u32[]{:S(2)}) async-start(bf16[16,28,2048]{2,1,0:T(8,128)(2,1)} %reshape.124), calls=%async_computation.2 | async-start | bytes 4194304 | tf_op jit(solution)/shard_map/all_to_all | solution.py:110
  31.0 3.5 %reshape.119 = bf16[16,28,2048]{2,1,0:T(8,128)(2,1)} reshape(bf16[448,2048]{1,0:T(8,128)(2,1)} %convolution_convert_fusion.4) | data formatting | bytes 3670016 | tf_op jit(solution)/shard_map/reshape | solution.py:65
  34.5 41.1 %all-to-all-done.2 = bf16[16,28,2048]{2,1,0:T(8,128)(2,1)S(1)} async-done(((bf16[16,28,2048]{2,1,0:T(8,128)(2,1)}), bf16[16,28,2048]{2,1,0:T(8,128)(2,1)S(1)}, u32[]{:S(2)}, u32[]{:S(2)}) %all-to-all-start.2) | async-done | bytes 1835040 | tf_op jit(solution)/shard_map/all_to_all | solution.py:110
  75.6 4.4 %all-to-all-start = ((bf16[16,28,2048]{2,1,0:T(8,128)(2,1)}), bf16[16,28,2048]{2,1,0:T(8,128)(2,1)}, u32[]{:S(2)}, u32[]{:S(2)}) async-start(bf16[16,28,2048]{2,1,0:T(8,128)(2,1)} %reshape.119), calls=%async_computation | async-start | bytes 4194304 | tf_op jit(solution)/shard_map/all_to_all | solution.py:66
  82.4 45.4 %all-to-all-done = bf16[16,28,2048]{2,1,0:T(8,128)(2,1)} async-done(((bf16[16,28,2048]{2,1,0:T(8,128)(2,1)}), bf16[16,28,2048]{2,1,0:T(8,128)(2,1)}, u32[]{:S(2)}, u32[]{:S(2)}) %all-to-all-start) | async-done | bytes 1835040 | tf_op jit(solution)/shard_map/all_to_all | solution.py:66
  127.8 3.6 %reshape.120 = bf16[448,2048]{1,0:T(8,128)(2,1)} reshape(bf16[16,28,2048]{2,1,0:T(8,128)(2,1)} %all-to-all-done) | data formatting | bytes 3670016 | tf_op jit(solution)/shard_map/reshape | solution.py:67
  131.4 4.6 %fusion = f32[448,768]{1,0:T(8,128)} fusion(bf16[448,2048]{1,0:T(8,128)(2,1)S(1)} %copy-done.4, bf16[1,2048,768]{2,1,0:T(8,128)(2,1)} %all-gather.11.cloned.1.call-done), kind=kOutput, calls=%fused_computation.7 | convolution fusion | flops 1409286144 | bytes 6356992 | tf_op jit(solution)/shard_map/dot_general | solution.py:122
  136.0 5.1 %fusion.6 = f32[448,768]{1,0:T(8,128)} fusion(bf16[448,2048]{1,0:T(8,128)(2,1)} %reshape.120, bf16[1,2048,768]{2,1,0:T(8,128)(2,1)} %all-gather.9.cloned.1.call-done), kind=kOutput, calls=%fused_computation.13 | convolution fusion | flops 1409286144 | bytes 6356992 | tf_op jit(solution)/shard_map/dot_general | solution.py:74
  141.1 7.3 %all-gather.7.cloned.1.call-done = bf16[1,2048,768]{2,1,0:T(8,128)(2,1)} async-done(((bf16[1,1024,768]{2,1,0:T(8,128)(2,1)}), bf16[1,2048,768]{2,1,0:T(8,128)(2,1)}) %all-gather.7.cloned.1.call-update) | async-done | bytes 3145744 | tf_op jit(solution)/shard_map/all_gather | solution.py:69
  148.4 5.3 %multiply_convert_fusion.2 = (bf16[448,768]{1,0:T(8,128)(2,1)S(1)}, bf16[448,768]{1,0:T(8,128)(2,1)S(1)}, bf16[448,768]{1,0:T(8,128)(2,1)S(1)}) fusion(f32[448,768]{1,0:T(8,128)} %fusion, f32[448,768]{1,0:T(8,128)} %fusion.6, bf16[448,2048]{1,0:T(8,128)(2,1)} %reshape.120, bf16[1,2048,768]{2,1,0:T(8,128)(2,1)} %all-gather.7.cloned.1.call-done), kind=kOutput, calls=%fused_computation.31 | convolution fusion | flops 1414447104 | bytes 9797632 | tf_op jit(solution)/shard_map/dot_general | solution.py:73
  159.5 4.5 %pad_maximum_fusion = bf16[2048,2304]{0,1:T(8,128)(2,1)} fusion(bf16[2048,768]{0,1:T(8,128)(2,1)S(1)} %convolution_convert_fusion, bf16[2048,768]{0,1:T(8,128)(2,1)S(1)} %convolution_convert_fusion.1, bf16[2048,768]{0,1:T(8,128)(2,1)S(1)} %convolution_convert_fusion.2), kind=kLoop, calls=%fused_computation.2 | loop fusion | flops 28311552 | bytes 18874368 | tf_op jit(solution)/shard_map/concatenate | solution.py:149
  164.6 3.7 %fusion.4 = f32[448,2048]{1,0:T(8,128)S(1)} fusion(bf16[448,768]{1,0:T(8,128)(2,1)S(1)} %get-tuple-element.41, bf16[1,2048,768]{2,1,0:T(8,128)(2,1)} %all-gather.9.cloned.1.call-done), kind=kOutput, calls=%fused_computation.11 | convolution fusion | flops 1409286144 | bytes 7503872 | tf_op jit(solution)/shard_map/dot_general | solution.py:26
  168.3 2.9 add_convert_fusion
  180.7 6.5 %all-to-all-start.1 = ((bf16[16,28,2048]{2,1,0:T(8,128)(2,1)}), bf16[16,28,2048]{2,1,0:T(8,128)(2,1)}, u32[]{:S(2)}, u32[]{:S(2)}) async-start(bf16[16,28,2048]{2,1,0:T(8,128)(2,1)} %reshape.121), calls=%async_computation.1 | async-start | bytes 4194304 | tf_op jit(solution)/shard_map/all_to_all | solution.py:79
  191.9 10.5 %collective-permute-done.1 = bf16[1,28,2048]{2,1,0:T(8,128)(2,1)S(1)} collective-permute-done((bf16[1,28,2048]{2,1,0:T(8,128)(2,1)S(1)}, bf16[1,28,2048]{2,1,0:T(8,128)(2,1)S(1)}, u32[]{:S(2)}, u32[]{:S(2)}) %collective-permute-start.1) | collective-permute-done | bytes 114720 | tf_op jit(solution)/shard_map/ppermute | solution.py:20
  202.3 3.9 %collective-permute-start.6 = (bf16[1,28,2048]{2,1,0:T(8,128)(2,1)S(1)}, bf16[1,28,2048]{2,1,0:T(8,128)(2,1)S(1)}, u32[]{:S(2)}, u32[]{:S(2)}) collective-permute-start(bf16[1,28,2048]{2,1,0:T(8,128)(2,1)S(1)} %get-tuple-element.51), channel_id=1, source_target_pairs={{0,7},{1,6},{2,5},{3,4},{4,3},{5,2},{6,1},{7,0},{8,15},{9,14},{10,... | collective-permute-start | bytes 344072 | tf_op jit(solution)/shard_map/ppermute | solution.py:20
  206.9 3.8 %collective-permute-start.7 = (bf16[1,28,2048]{2,1,0:T(8,128)(2,1)S(1)}, bf16[1,28,2048]{2,1,0:T(8,128)(2,1)S(1)}, u32[]{:S(2)}, u32[]{:S(2)}) collective-permute-start(bf16[1,28,2048]{2,1,0:T(8,128)(2,1)S(1)} %get-tuple-element.50), channel_id=1, source_target_pairs={{0,8},{1,9},{2,10},{3,11},{4,12},{5,13},{6,14},{7,15},{8,0},{9,1},... | collective-permute-start | bytes 344072 | tf_op jit(solution)/shard_map/ppermute | solution.py:20
  211.4 14.2 %collective-permute-done.3 = bf16[1,28,2048]{2,1,0:T(8,128)(2,1)S(1)} collective-permute-done((bf16[1,28,2048]{2,1,0:T(8,128)(2,1)S(1)}, bf16[1,28,2048]{2,1,0:T(8,128)(2,1)S(1)}, u32[]{:S(2)}, u32[]{:S(2)}) %collective-permute-start.3) | collective-permute-done | bytes 114720 | tf_op jit(solution)/shard_map/ppermute | solution.py:20
  231.0 3.9 %collective-permute-start.10 = (bf16[1,28,2048]{2,1,0:T(8,128)(2,1)S(1)}, bf16[1,28,2048]{2,1,0:T(8,128)(2,1)S(1)}, u32[]{:S(2)}, u32[]{:S(2)}) collective-permute-start(bf16[1,28,2048]{2,1,0:T(8,128)(2,1)S(1)} %get-tuple-element.47), channel_id=1, source_target_pairs={{0,11},{1,10},{2,9},{3,8},{4,15},{5,14},{6,13},{7,12},{8,3},{9,2},... | collective-permute-start | bytes 344072 | tf_op jit(solution)/shard_map/ppermute | solution.py:20
  237.2 13.2 %collective-permute-done.7 = bf16[1,28,2048]{2,1,0:T(8,128)(2,1)S(1)} collective-permute-done((bf16[1,28,2048]{2,1,0:T(8,128)(2,1)S(1)}, bf16[1,28,2048]{2,1,0:T(8,128)(2,1)S(1)}, u32[]{:S(2)}, u32[]{:S(2)}) %collective-permute-start.7) | collective-permute-done | bytes 114720 | tf_op jit(solution)/shard_map/ppermute | solution.py:20
  255.0 6.7 %collective-permute-done.9 = bf16[1,28,2048]{2,1,0:T(8,128)(2,1)S(1)} collective-permute-done((bf16[1,28,2048]{2,1,0:T(8,128)(2,1)S(1)}, bf16[1,28,2048]{2,1,0:T(8,128)(2,1)S(1)}, u32[]{:S(2)}, u32[]{:S(2)}) %collective-permute-start.9) | collective-permute-done | bytes 114720 | tf_op jit(solution)/shard_map/ppermute | solution.py:20
  265.3 3.8 %collective-permute-done.11 = bf16[1,28,2048]{2,1,0:T(8,128)(2,1)S(1)} collective-permute-done((bf16[1,28,2048]{2,1,0:T(8,128)(2,1)S(1)}, bf16[1,28,2048]{2,1,0:T(8,128)(2,1)S(1)}, u32[]{:S(2)}, u32[]{:S(2)}) %collective-permute-start.11) | collective-permute-done | bytes 114720 | tf_op jit(solution)/shard_map/ppermute | solution.py:20
  269.8 5.7 %collective-permute-done.12 = bf16[1,28,2048]{2,1,0:T(8,128)(2,1)S(1)} collective-permute-done((bf16[1,28,2048]{2,1,0:T(8,128)(2,1)S(1)}, bf16[1,28,2048]{2,1,0:T(8,128)(2,1)S(1)}, u32[]{:S(2)}, u32[]{:S(2)}) %collective-permute-start.12) | collective-permute-done | bytes 114720 | tf_op jit(solution)/shard_map/ppermute | solution.py:20
  290.8 4.2 %multiply_reduce_fusion = (f32[256]{0:T(256)S(1)}, f32[256,2048]{1,0:T(8,128)}, f32[256,2048]{1,0:T(8,128)S(1)}) fusion(f32[256,2048]{1,0:T(8,128)} %copy-done.2, f32[256]{0:T(256)S(1)} %get-tuple-element.63, bf16[256,2048]{1,0:T(8,128)(2,1)} %gather_fusion, pred[256]{0:T(512)(128)(4,1)S(1)} %copy-done.11, f32[256]{0:T(256)S(1)} %mul.91, ...), kind=kLoop, calls=%fused_computation.22 | loop fusion | flops 4718336 | bytes 8391936 | tf_op jit(solution)/shard_map/reduce_sum | solution.py:102
  295.0 3.5 %reshape.123 = f32[128,2,2048]{2,1,0:T(2,128)} reshape(f32[256,2048]{1,0:T(8,128)} %get-tuple-element.60) | data formatting | bytes 4194304 | tf_op jit(solution)/shard_map/reshape | solution.py:98
  300.7 5.1 %reduce_sum.72 = bf16[128,2048]{1,0:T(8,128)(2,1)} reduce(f32[128,2,2048]{2,1,0:T(2,128)} %reshape.123, f32[]{:T(128)} %constant.10.clone.1), dimensions={1}, to_apply=%region_6.8 | reduce | flops 262144 | bytes 2621444 | tf_op jit(solution)/shard_map/reduce_sum | solution.py:99
  305.9 3.8 %reduce_sum.73 = bf16[128,2048]{1,0:T(8,128)(2,1)} reduce(f32[128,2,2048]{2,1,0:T(2,128)S(1)} %copy-done.3, f32[]{:T(128)} %constant.10.clone.1), dimensions={1}, to_apply=%region_7.9 | reduce | flops 262144 | bytes 2621444 | tf_op jit(solution)/shard_map/reduce_sum | solution.py:146
  310.4 4.5 %slice_bitcast_fusion = (bf16[1,1024,768]{1,2,0:T(8,128)(2,1)S(1)}, bf16[1,1024,768]{1,2,0:T(8,128)(2,1)}, bf16[1,1024,768]{1,2,0:T(8,128)(2,1)}) fusion(bf16[1024,2304]{0,1:T(8,128)(2,1)} %reduce-scatter.2.cloned.1.call-done), kind=kLoop, calls=%fused_computation.27 | loop fusion | bytes 9437184 | tf_op jit(solution)/shard_map/broadcast_in_dim | solution.py:163
  314.9 2.6 copy.46
  317.5 2.6 copy.47
  (129 shorter events, 71.3 us)
Async XLA Ops:
  7.2 21.9 %copy-start = (bf16[128,2048]{1,0:T(8,128)(2,1)S(1)}, bf16[128,2048]{1,0:T(8,128)(2,1)}, u32[]{:S(2)}) copy-start(bf16[128,2048]{1,0:T(8,128)(2,1)} %param.10) | copy-start | bytes 1572868
  7.2 124.2 %all-gather.11.cloned.1.call-start = ((), (), s32[]{:S(2)}) async-start(), calls=%async_computation.7 | async-start | bytes 4718592 | tf_op jit(solution)/shard_map/all_gather | solution.py:77
  14.1 7.0 %copy-start.2 = (f32[256,2048]{1,0:T(8,128)}, f32[256,2048]{1,0:T(8,128)S(1)}, u32[]{:S(2)}) copy-start(f32[256,2048]{1,0:T(8,128)S(1)} %convert_element_type.84) | copy-start | bytes 6291460
  21.1 7.9 %copy-start.10 = (s32[128,2]{0,1:T(2,128)S(1)}, s32[128,2]{0,1:T(2,128)}, u32[]{:S(2)}) copy-start(s32[128,2]{0,1:T(2,128)} %param.12) | copy-start | bytes 3076
  21.1 54.5 %all-to-all-start.2 = ((bf16[16,28,2048]{2,1,0:T(8,128)(2,1)}), bf16[16,28,2048]{2,1,0:T(8,128)(2,1)S(1)}, u32[]{:S(2)}, u32[]{:S(2)}) async-start(bf16[16,28,2048]{2,1,0:T(8,128)(2,1)} %reshape.124), calls=%async_computation.2 | async-start | bytes 4194304 | tf_op jit(solution)/shard_map/all_to_all | solution.py:110
  27.8 108.2 %all-gather.9.cloned.1.call-start = ((), (), s32[]{:S(2)}) async-start(), calls=%async_computation.6 | async-start | bytes 4718592 | tf_op jit(solution)/shard_map/all_gather | solution.py:70
  75.6 52.2 %all-to-all-start = ((bf16[16,28,2048]{2,1,0:T(8,128)(2,1)}), bf16[16,28,2048]{2,1,0:T(8,128)(2,1)}, u32[]{:S(2)}, u32[]{:S(2)}) async-start(bf16[16,28,2048]{2,1,0:T(8,128)(2,1)} %reshape.119), calls=%async_computation | async-start | bytes 4194304 | tf_op jit(solution)/shard_map/all_to_all | solution.py:66
  80.0 68.4 %all-gather.7.cloned.1.call-start = ((), (), s32[]{:S(2)}) async-start(), calls=%async_computation.5 | async-start | bytes 4718592 | tf_op jit(solution)/shard_map/all_gather | solution.py:69
  80.7 229.7 %reduce-scatter.2.cloned.1.call-start = ((), (), s32[]{:S(2)}) async-start(), calls=%async_computation.4 | async-start | bytes 14155776 | tf_op jit(solution)/shard_map/reduce_scatter | solution.py:148
  82.4 49.0 %copy-start.4 = (bf16[448,2048]{1,0:T(8,128)(2,1)S(1)}, bf16[448,2048]{1,0:T(8,128)(2,1)}, u32[]{:S(2)}) copy-start(bf16[448,2048]{1,0:T(8,128)(2,1)} %reshape.125) | copy-start | bytes 5505028
  153.7 3.9 %copy-start.18 = (bf16[448,768]{1,0:T(8,128)(2,1)}, bf16[448,768]{1,0:T(8,128)(2,1)S(1)}, u32[]{:S(2)}) copy-start(bf16[448,768]{1,0:T(8,128)(2,1)S(1)} %get-tuple-element.40) | copy-start | bytes 2064388
  176.2 14.6 %collective-permute-start = (bf16[1,28,2048]{2,1,0:T(8,128)(2,1)}, bf16[1,28,2048]{2,1,0:T(8,128)(2,1)S(1)}, u32[]{:S(2)}, u32[]{:S(2)}) collective-permute-start(bf16[1,28,2048]{2,1,0:T(8,128)(2,1)} %get-tuple-element.57), channel_id=1, source_target_pairs={{0,1},{1,0},{2,3},{3,2},{4,5},{5,4},{6,7},{7,6},{8,9},{9,8},{10,11... | collective-permute-start | bytes 344072 | tf_op jit(solution)/shard_map/ppermute | solution.py:20
  180.7 6.5 %copy-start.9 = (bf16[1,28,2048]{2,1,0:T(8,128)(2,1)S(1)}, bf16[1,28,2048]{2,1,0:T(8,128)(2,1)}, u32[]{:S(2)}) copy-start(bf16[1,28,2048]{2,1,0:T(8,128)(2,1)} %get-tuple-element.56) | copy-start | bytes 344068
  180.7 6.9 %copy-start.8 = (bf16[1,28,2048]{2,1,0:T(8,128)(2,1)S(1)}, bf16[1,28,2048]{2,1,0:T(8,128)(2,1)}, u32[]{:S(2)}) copy-start(bf16[1,28,2048]{2,1,0:T(8,128)(2,1)} %get-tuple-element.55) | copy-start | bytes 344068
  180.7 8.6 %copy-start.7 = (bf16[1,28,2048]{2,1,0:T(8,128)(2,1)S(1)}, bf16[1,28,2048]{2,1,0:T(8,128)(2,1)}, u32[]{:S(2)}) copy-start(bf16[1,28,2048]{2,1,0:T(8,128)(2,1)} %get-tuple-element.54) | copy-start | bytes 344068
  180.7 105.3 %all-to-all-start.1 = ((bf16[16,28,2048]{2,1,0:T(8,128)(2,1)}), bf16[16,28,2048]{2,1,0:T(8,128)(2,1)}, u32[]{:S(2)}, u32[]{:S(2)}) async-start(bf16[16,28,2048]{2,1,0:T(8,128)(2,1)} %reshape.121), calls=%async_computation.1 | async-start | bytes 4194304 | tf_op jit(solution)/shard_map/all_to_all | solution.py:79
  187.3 15.0 %collective-permute-start.1 = (bf16[1,28,2048]{2,1,0:T(8,128)(2,1)S(1)}, bf16[1,28,2048]{2,1,0:T(8,128)(2,1)S(1)}, u32[]{:S(2)}, u32[]{:S(2)}) collective-permute-start(bf16[1,28,2048]{2,1,0:T(8,128)(2,1)S(1)} %copy-done.9), channel_id=1, source_target_pairs={{0,2},{1,3},{2,0},{3,1},{4,6},{5,7},{6,4},{7,5},{8,10},{9,11},{10,... | collective-permute-start | bytes 344072 | tf_op jit(solution)/shard_map/ppermute | solution.py:20
  187.6 19.3 %collective-permute-start.2 = (bf16[1,28,2048]{2,1,0:T(8,128)(2,1)S(1)}, bf16[1,28,2048]{2,1,0:T(8,128)(2,1)S(1)}, u32[]{:S(2)}, u32[]{:S(2)}) collective-permute-start(bf16[1,28,2048]{2,1,0:T(8,128)(2,1)S(1)} %copy-done.8), channel_id=1, source_target_pairs={{0,3},{1,2},{2,1},{3,0},{4,7},{5,6},{6,5},{7,4},{8,11},{9,10},{10,... | collective-permute-start | bytes 344072 | tf_op jit(solution)/shard_map/ppermute | solution.py:20
  189.4 36.2 %collective-permute-start.3 = (bf16[1,28,2048]{2,1,0:T(8,128)(2,1)S(1)}, bf16[1,28,2048]{2,1,0:T(8,128)(2,1)S(1)}, u32[]{:S(2)}, u32[]{:S(2)}) collective-permute-start(bf16[1,28,2048]{2,1,0:T(8,128)(2,1)S(1)} %copy-done.7), channel_id=1, source_target_pairs={{0,4},{1,5},{2,6},{3,7},{4,0},{5,1},{6,2},{7,3},{8,12},{9,13},{10,... | collective-permute-start | bytes 344072 | tf_op jit(solution)/shard_map/ppermute | solution.py:20
  189.7 39.8 %collective-permute-start.4 = (bf16[1,28,2048]{2,1,0:T(8,128)(2,1)S(1)}, bf16[1,28,2048]{2,1,0:T(8,128)(2,1)S(1)}, u32[]{:S(2)}, u32[]{:S(2)}) collective-permute-start(bf16[1,28,2048]{2,1,0:T(8,128)(2,1)S(1)} %get-tuple-element.53), channel_id=1, source_target_pairs={{0,5},{1,4},{2,7},{3,6},{4,1},{5,0},{6,3},{7,2},{8,13},{9,12},{10,... | collective-permute-start | bytes 344072 | tf_op jit(solution)/shard_map/ppermute | solution.py:20
  190.9 40.2 %collective-permute-start.5 = (bf16[1,28,2048]{2,1,0:T(8,128)(2,1)S(1)}, bf16[1,28,2048]{2,1,0:T(8,128)(2,1)S(1)}, u32[]{:S(2)}, u32[]{:S(2)}) collective-permute-start(bf16[1,28,2048]{2,1,0:T(8,128)(2,1)S(1)} %get-tuple-element.52), channel_id=1, source_target_pairs={{0,6},{1,7},{2,4},{3,5},{4,2},{5,3},{6,0},{7,1},{8,14},{9,15},{10,... | collective-permute-start | bytes 344072 | tf_op jit(solution)/shard_map/ppermute | solution.py:20
  202.3 33.5 %collective-permute-start.6 = (bf16[1,28,2048]{2,1,0:T(8,128)(2,1)S(1)}, bf16[1,28,2048]{2,1,0:T(8,128)(2,1)S(1)}, u32[]{:S(2)}, u32[]{:S(2)}) collective-permute-start(bf16[1,28,2048]{2,1,0:T(8,128)(2,1)S(1)} %get-tuple-element.51), channel_id=1, source_target_pairs={{0,7},{1,6},{2,5},{3,4},{4,3},{5,2},{6,1},{7,0},{8,15},{9,14},{10,... | collective-permute-start | bytes 344072 | tf_op jit(solution)/shard_map/ppermute | solution.py:20
  206.9 43.5 %collective-permute-start.7 = (bf16[1,28,2048]{2,1,0:T(8,128)(2,1)S(1)}, bf16[1,28,2048]{2,1,0:T(8,128)(2,1)S(1)}, u32[]{:S(2)}, u32[]{:S(2)}) collective-permute-start(bf16[1,28,2048]{2,1,0:T(8,128)(2,1)S(1)} %get-tuple-element.50), channel_id=1, source_target_pairs={{0,8},{1,9},{2,10},{3,11},{4,12},{5,13},{6,14},{7,15},{8,0},{9,1},... | collective-permute-start | bytes 344072 | tf_op jit(solution)/shard_map/ppermute | solution.py:20
  225.5 27.9 %collective-permute-start.8 = (bf16[1,28,2048]{2,1,0:T(8,128)(2,1)S(1)}, bf16[1,28,2048]{2,1,0:T(8,128)(2,1)S(1)}, u32[]{:S(2)}, u32[]{:S(2)}) collective-permute-start(bf16[1,28,2048]{2,1,0:T(8,128)(2,1)S(1)} %get-tuple-element.49), channel_id=1, source_target_pairs={{0,9},{1,8},{2,11},{3,10},{4,13},{5,12},{6,15},{7,14},{8,1},{9,0},... | collective-permute-start | bytes 344072 | tf_op jit(solution)/shard_map/ppermute | solution.py:20
  229.5 32.1 %collective-permute-start.9 = (bf16[1,28,2048]{2,1,0:T(8,128)(2,1)S(1)}, bf16[1,28,2048]{2,1,0:T(8,128)(2,1)S(1)}, u32[]{:S(2)}, u32[]{:S(2)}) collective-permute-start(bf16[1,28,2048]{2,1,0:T(8,128)(2,1)S(1)} %get-tuple-element.48), channel_id=1, source_target_pairs={{0,10},{1,11},{2,8},{3,9},{4,14},{5,15},{6,12},{7,13},{8,2},{9,3},... | collective-permute-start | bytes 344072 | tf_op jit(solution)/shard_map/ppermute | solution.py:20
  231.0 33.6 %collective-permute-start.10 = (bf16[1,28,2048]{2,1,0:T(8,128)(2,1)S(1)}, bf16[1,28,2048]{2,1,0:T(8,128)(2,1)S(1)}, u32[]{:S(2)}, u32[]{:S(2)}) collective-permute-start(bf16[1,28,2048]{2,1,0:T(8,128)(2,1)S(1)} %get-tuple-element.47), channel_id=1, source_target_pairs={{0,11},{1,10},{2,9},{3,8},{4,15},{5,14},{6,13},{7,12},{8,3},{9,2},... | collective-permute-start | bytes 344072 | tf_op jit(solution)/shard_map/ppermute | solution.py:20
  235.8 33.3 %collective-permute-start.11 = (bf16[1,28,2048]{2,1,0:T(8,128)(2,1)S(1)}, bf16[1,28,2048]{2,1,0:T(8,128)(2,1)S(1)}, u32[]{:S(2)}, u32[]{:S(2)}) collective-permute-start(bf16[1,28,2048]{2,1,0:T(8,128)(2,1)S(1)} %get-tuple-element.46), channel_id=1, source_target_pairs={{0,12},{1,13},{2,14},{3,15},{4,8},{5,9},{6,10},{7,11},{8,4},{9,5},... | collective-permute-start | bytes 344072 | tf_op jit(solution)/shard_map/ppermute | solution.py:20
  250.4 25.1 %collective-permute-start.12 = (bf16[1,28,2048]{2,1,0:T(8,128)(2,1)S(1)}, bf16[1,28,2048]{2,1,0:T(8,128)(2,1)S(1)}, u32[]{:S(2)}, u32[]{:S(2)}) collective-permute-start(bf16[1,28,2048]{2,1,0:T(8,128)(2,1)S(1)} %get-tuple-element.45), channel_id=1, source_target_pairs={{0,13},{1,12},{2,15},{3,14},{4,9},{5,8},{6,11},{7,10},{8,5},{9,4},... | collective-permute-start | bytes 344072 | tf_op jit(solution)/shard_map/ppermute | solution.py:20
  253.4 24.1 %collective-permute-start.13 = (bf16[1,28,2048]{2,1,0:T(8,128)(2,1)S(1)}, bf16[1,28,2048]{2,1,0:T(8,128)(2,1)S(1)}, u32[]{:S(2)}, u32[]{:S(2)}) collective-permute-start(bf16[1,28,2048]{2,1,0:T(8,128)(2,1)S(1)} %get-tuple-element.44), channel_id=1, source_target_pairs={{0,14},{1,15},{2,12},{3,13},{4,10},{5,11},{6,8},{7,9},{8,6},{9,7},... | collective-permute-start | bytes 344072 | tf_op jit(solution)/shard_map/ppermute | solution.py:20
  261.6 19.0 %collective-permute-start.14 = (bf16[1,28,2048]{2,1,0:T(8,128)(2,1)S(1)}, bf16[1,28,2048]{2,1,0:T(8,128)(2,1)S(1)}, u32[]{:S(2)}, u32[]{:S(2)}) collective-permute-start(bf16[1,28,2048]{2,1,0:T(8,128)(2,1)S(1)} %get-tuple-element.43), channel_id=1, source_target_pairs={{0,15},{1,14},{2,13},{3,12},{4,11},{5,10},{6,9},{7,8},{8,7},{9,6},... | collective-permute-start | bytes 344072 | tf_op jit(solution)/shard_map/ppermute | solution.py:20
  300.7 5.1 %copy-start.3 = (f32[128,2,2048]{2,1,0:T(2,128)S(1)}, f32[128,2,2048]{2,1,0:T(2,128)}, u32[]{:S(2)}) copy-start(f32[128,2,2048]{2,1,0:T(2,128)} %reshape.128) | copy-start | bytes 6291460
  317.5 4.2 %copy-start.1 = (bf16[128,2048]{1,0:T(8,128)(2,1)S(1)}, bf16[128,2048]{1,0:T(8,128)(2,1)}, u32[]{:S(2)}) copy-start(bf16[128,2048]{1,0:T(8,128)(2,1)} %param.10) | copy-start | bytes 1572868
  (10 other events, 27.2 us)
Sparse Core Ops, SparseCore 0:
  9.5 45.8 all-gather.10
  57.0 44.8 all-gather.8
  103.5 44.8 all-gather.6
  164.1 110.6 reduce-scatter.1
